TPU v7x, 128 devices: a whole 4x4x4 slice. The times are simulated.
128 devices in a mesh: layer: 4 (over z_lo, core), row: 8 (over z_hi, y), col: 4 (over x).
Axes of the slice: x: 4, y: 4, z: 4 (z_hi: 2, z_lo: 2; z = z_hi * 2 + z_lo), core: 2. Of those that a mesh axis runs over, the one named last changes fastest.
Arguments:
- grad: bfloat16 [32768, 8192], P(('layer', 'row'), 'col'), parts along dimension 0, may hold values from -6 to 6
- error: bfloat16 [32768, 8192], P(('layer', 'row'), 'col'), parts along dimension 0, may hold values from -2 to 2
- left_old: bfloat16 [32768, 512], P(('layer', 'row')), parts along dimension 0, may hold values from -0.25 to 0.25
- right_old: bfloat16 [32768, 512], P(('layer', 'col')), parts along dimension 0, may hold values from -0.25 to 0.25
- first_old: float32 [2048, 512], P('layer'), parts along dimension 0, may hold values from -3 to 3
- second_old: float32 [2048, 512], P('layer'), parts along dimension 0, may hold values from 0.05 to 1
Outputs:
- error_new: bfloat16 [32768, 8192], P(('layer', 'row'), 'col'), parts along dimension 0
- first_moment: float32 [2048, 512], P('layer'), parts along dimension 0
- second_moment: float32 [2048, 512], P('layer'), parts along dimension 0
- update: float32 [2048, 512], P('layer'), parts along dimension 0
There are 4 independent parts, one for each index of `layer`. A program takes and returns all parts, laid end to end along the dimension named above; each array names one. Nothing has to cross between parts.
All inputs are finite; a program needn't handle non-finite values.
Results may differ from a plain program's by a relative error of at most 0.0075.
Values may be sent and summed in bfloat16 or wider, within the bound.
No kernel may reach another device: no remote copies, remote signals or barrier semaphores. Data moves between devices by JAX's collectives and lax.ppermute only.
A program may use at most 128 MiB of HBM per device.

v0:
```python
import jax
import jax.numpy as jnp
from jax import lax
from jax.sharding import PartitionSpec as P


def solve_rows(image, gram):
    factor = jnp.linalg.cholesky(gram)
    return jax.scipy.linalg.solve_triangular(factor, image.T, lower=True).T.astype(jnp.bfloat16)


def gram_of(image):
    return lax.dot_general(image, image, (((0,), (0,)), ((), ())), precision=lax.Precision.HIGH)


def split_pair(values):
    upper = values.astype(jnp.bfloat16)
    lower = (values - upper.astype(jnp.float32)).astype(jnp.bfloat16)
    return (upper, lower)


def per_device(grad, error, left_old, right_old, first_old, second_old):
    highest = lax.Precision.HIGHEST
    across = (((0,), (0,)), ((), ()))
    left_image = lax.psum(jnp.dot(grad, right_old, preferred_element_type=jnp.float32), "col")
    left_gram = lax.psum(gram_of(left_image), "row")
    left_basis = solve_rows(left_image, left_gram)
    right_part = lax.dot_general(grad, left_basis, across, preferred_element_type=jnp.float32)
    right_image = lax.psum(right_part, "row")
    right_gram = lax.psum(gram_of(right_image), "col")
    right_basis = solve_rows(right_image, right_gram)
    summed = grad.astype(jnp.float32) + error.astype(jnp.float32)
    accum = summed.astype(jnp.bfloat16)
    carried = jnp.dot(accum, right_basis, preferred_element_type=jnp.float32)
    carried_upper, carried_lower = split_pair(carried)
    core_part = lax.dot_general(
        left_basis, carried_upper, across, preferred_element_type=jnp.float32
    ) + lax.dot_general(left_basis, carried_lower, across, preferred_element_type=jnp.float32)
    left_count = left_basis.shape[0] // lax.axis_size("col")
    left_start = lax.axis_index("col") * left_count
    left_piece = lax.dynamic_slice_in_dim(left_basis, left_start, left_count, 0)
    left_prior = lax.dynamic_slice_in_dim(left_old, left_start, left_count, 0)
    right_count = right_basis.shape[0] // lax.axis_size("row")
    right_start = lax.axis_index("row") * right_count
    right_piece = lax.dynamic_slice_in_dim(right_basis, right_start, right_count, 0)
    right_prior = lax.dynamic_slice_in_dim(right_old, right_start, right_count, 0)
    turn_left_part = lax.dot_general(
        left_piece, left_prior, across, preferred_element_type=jnp.float32
    )
    turn_right_part = lax.dot_general(
        right_piece, right_prior, across, preferred_element_type=jnp.float32
    )
    core, turn_left, turn_right = lax.psum(
        (core_part, turn_left_part, turn_right_part), ("row", "col")
    )
    core_upper, core_lower = split_pair(core)
    lifted_full = jnp.dot(left_basis, core_upper, preferred_element_type=jnp.float32) + jnp.dot(
        left_basis, core_lower, preferred_element_type=jnp.float32
    )
    lifted = lifted_full.astype(jnp.bfloat16)
    rebuilt = lax.dot_general(
        lifted, right_basis, (((1,), (1,)), ((), ())), preferred_element_type=jnp.float32
    )
    error_new = (summed - rebuilt).astype(jnp.bfloat16)
    first_turned = jnp.dot(
        jnp.dot(turn_left, first_old, precision=highest), turn_right.T, precision=highest
    )
    excess = jnp.maximum(second_old - first_old * first_old, 0.0)
    second_turned = (
        jnp.dot(
            jnp.dot(turn_left * turn_left, excess, precision=highest),
            (turn_right * turn_right).T,
            precision=highest,
        )
        + first_turned * first_turned
    )
    first_moment = 0.9 * first_turned + 0.1 * core
    second_moment = 0.999 * second_turned + 0.001 * core * core
    update = first_moment / (jnp.sqrt(second_moment) + 0.01)
    return (error_new, first_moment, second_moment, update)


def solution(mesh):
    return jax.shard_map(
        per_device,
        mesh=mesh,
        in_specs=(
            P(("layer", "row"), "col"),
            P(("layer", "row"), "col"),
            P(("layer", "row"), None),
            P(("layer", "col"), None),
            P("layer", None),
            P("layer", None),
        ),
        out_specs=(
            P(("layer", "row"), "col"),
            P("layer", None),
            P("layer", None),
            P("layer", None),
        ),
        check_vma=False,
    )
```

profile of v0, /device:TPU:0, one launch (start us, length us, event | category | flops | bytes accessed | tf_op | source)
XLA Modules:
  0.0 1060.0 jit_solution(5173255046993698777)
XLA Ops:
  14.7 61.2 %all-reduce.8.cloned.1.call-done = f32[1024,512]{1,0:T(8,128)} async-done(((f32[1024,512]{1,0:T(8,128)}), f32[1024,512]{1,0:T(8,128)}) %all-reduce.8.cloned.1.call-update) | async-done | bytes 2097168 | tf_op jit(solution)/shard_map/psum | solution.py:25
  81.4 87.5 %all-reduce.10.cloned.1.call-done = f32[512,512]{0,1:T(8,128)} async-done(((f32[512,512]{0,1:T(8,128)}), f32[512,512]{0,1:T(8,128)}) %all-reduce.10.cloned.1.call-update) | async-done | bytes 1048592 | tf_op jit(solution)/shard_map/psum | solution.py:26
  174.0 11.7 %cholesky.286 = f32[128,128]{1,0:T(8,128)S(1)} custom-call(f32[128,128]{1,0:T(8,128)S(1)} %cholesky.426), custom_call_target="Cholesky" | custom-call | tf_op jit(solution)/shard_map/jit(cholesky)/cholesky | solution.py:8
  185.8 9.8 custom-call.33
  198.2 11.7 %cholesky.305 = f32[128,128]{1,0:T(8,128)S(1)} custom-call(f32[128,128]{1,0:T(8,128)S(1)} %cholesky.430), custom_call_target="Cholesky" | custom-call | tf_op jit(solution)/shard_map/jit(cholesky)/cholesky | solution.py:8
  209.9 10.0 custom-call.34
  221.5 11.7 %cholesky.326 = f32[128,128]{1,0:T(8,128)S(1)} custom-call(f32[128,128]{1,0:T(8,128)S(1)} %cholesky.435), custom_call_target="Cholesky" | custom-call | tf_op jit(solution)/shard_map/jit(cholesky)/cholesky | solution.py:8
  233.2 9.8 custom-call.35
  244.5 11.7 %cholesky.343 = f32[128,128]{1,0:T(8,128)S(1)} custom-call(f32[128,128]{1,0:T(8,128)S(1)} %convolution_subtract_fusion.9), custom_call_target="Cholesky" | custom-call | tf_op jit(solution)/shard_map/jit(cholesky)/cholesky | solution.py:8
  262.1 11.6 %while.2 = (s32[]{:T(128)}, f32[512,512]{1,0:T(8,128)}, s32[4,2]{0,1:T(2,128)S(1)}, f32[4,128,128]{2,1,0:T(8,128)S(1)}, s32[]{:T(128)}) while((s32[]{:T(128)}, f32[512,512]{1,0:T(8,128)}, s32[4,2]{0,1:T(2,128)S(1)}, f32[4,128,128]{2,1,0:T(8,128)S(1)}, s32[]{:T(128)}) %tuple.61), condition=%wide.while_cond, body=%wide.while_body.sunk | while | flops 2 | bytes 131189 | solution.py:9
  273.7 39.3 %custom-call.28 = f32[4,128,128]{1,2,0:T(8,128)S(1)} custom-call(f32[4,128,128]{2,1,0:T(8,128)S(1)} %get-tuple-element.12), custom_call_target="InvertDiagBlocksLowerTriangular" | custom-call | tf_op jit(solution)/shard_map/jit(_solve_triangular)/triangular_solve | solution.py:9
  330.4 108.0 %all-reduce.12.cloned.1.call-done = f32[2048,512]{0,1:T(8,128)} async-done(((f32[2048,512]{0,1:T(8,128)}), f32[2048,512]{0,1:T(8,128)}) %all-reduce.12.cloned.1.call-update) | async-done | bytes 4194320 | tf_op jit(solution)/shard_map/psum | solution.py:29
  448.8 42.1 %all-reduce.14.cloned.1.call-done = f32[512,512]{0,1:T(8,128)} async-done(((f32[512,512]{0,1:T(8,128)}), f32[512,512]{0,1:T(8,128)}) %all-reduce.14.cloned.1.call-update) | async-done | bytes 1048592 | tf_op jit(solution)/shard_map/psum | solution.py:30
  496.0 11.7 %cholesky.358 = f32[128,128]{1,0:T(8,128)S(1)} custom-call(f32[128,128]{1,0:T(8,128)S(1)} %cholesky.439), custom_call_target="Cholesky" | custom-call | tf_op jit(solution)/shard_map/jit(cholesky)/cholesky | solution.py:8
  507.9 9.8 custom-call.36
  520.9 11.7 %cholesky.377 = f32[128,128]{1,0:T(8,128)S(1)} custom-call(f32[128,128]{1,0:T(8,128)S(1)} %cholesky.443), custom_call_target="Cholesky" | custom-call | tf_op jit(solution)/shard_map/jit(cholesky)/cholesky | solution.py:8
  532.6 10.2 custom-call.37
  545.9 13.2 %cholesky.398 = f32[128,128]{1,0:T(8,128)} custom-call(f32[128,128]{1,0:T(8,128)} %cholesky.448), custom_call_target="Cholesky" | custom-call | tf_op jit(solution)/shard_map/jit(cholesky)/cholesky | solution.py:8
  560.6 11.3 %custom-call.38 = f32[1,128,128]{1,2,0:T(8,128)} custom-call(f32[1,128,128]{2,1,0:T(8,128)} %get-tuple-element.49), custom_call_target="InvertDiagBlocksLowerTriangular" | custom-call | tf_op jit(solution)/shard_map/jit(cholesky)/cholesky | solution.py:8
  574.1 11.9 %cholesky.415 = f32[128,128]{1,0:T(8,128)S(1)} custom-call(f32[128,128]{1,0:T(8,128)S(1)} %convolution_subtract_fusion.8), custom_call_target="Cholesky" | custom-call | tf_op jit(solution)/shard_map/jit(cholesky)/cholesky | solution.py:8
  592.2 11.6 %while.3 = (s32[]{:T(128)}, f32[512,512]{1,0:T(8,128)}, s32[4,2]{0,1:T(2,128)S(1)}, f32[4,128,128]{2,1,0:T(8,128)S(1)}, s32[]{:T(128)}) while((s32[]{:T(128)}, f32[512,512]{1,0:T(8,128)}, s32[4,2]{0,1:T(2,128)S(1)}, f32[4,128,128]{2,1,0:T(8,128)S(1)}, s32[]{:T(128)}) %tuple.78), condition=%wide.while_cond.1, body=%wide.while_body.1.sunk | while | flops 2 | bytes 131189 | solution.py:9
  603.8 39.3 %custom-call.29 = f32[4,128,128]{1,2,0:T(8,128)S(1)} custom-call(f32[4,128,128]{2,1,0:T(8,128)S(1)} %get-tuple-element.20), custom_call_target="InvertDiagBlocksLowerTriangular" | custom-call | tf_op jit(solution)/shard_map/jit(_solve_triangular)/triangular_solve | solution.py:9
  665.1 362.9 %all-reduce.16.cloned.1.call-done = (f32[512,512]{1,0:T(8,128)}, f32[512,512]{1,0:T(8,128)}, f32[512,512]{1,0:T(8,128)}) async-done(((f32[512,512]{1,0:T(8,128)}, f32[512,512]{1,0:T(8,128)}, f32[512,512]{1,0:T(8,128)}), (f32[512,512]{1,0:T(8,128)}, f32[512,512]{1,0:T(8,128)}, f32[512,512]{1,0:T(8,128)})) %all-reduce.16.cloned.1.call-update) | async-done | bytes 3145744 | tf_op jit(solution)/shard_map/psum | solution.py:53
  1031.6 10.4 subtract_convert_fusion
  (161 shorter events, 133.2 us)
Async XLA Ops:
  7.2 68.7 %all-reduce.8.cloned.1.call-start = ((), (), s32[]{:S(2)}) async-start(), calls=%async_computation | async-start | bytes 4194304 | tf_op jit(solution)/shard_map/psum | solution.py:25
  14.6 154.3 %all-reduce.10.cloned.1.call-start = ((), (), s32[]{:S(2)}) async-start(), calls=%async_computation.1 | async-start | bytes 2097152 | tf_op jit(solution)/shard_map/psum | solution.py:26
  80.9 357.4 %all-reduce.12.cloned.1.call-start = ((), (), s32[]{:S(2)}) async-start(), calls=%async_computation.2 | async-start | bytes 8388608 | tf_op jit(solution)/shard_map/psum | solution.py:29
  168.9 2.6 copy-start.5
  313.0 4.7 copy-start.2
  314.9 131.6 %copy-start.16 = (bf16[128,1024]{1,0:T(8,128)(2,1)}, bf16[128,1024]{1,0:T(8,128)(2,1)S(1)}, u32[]{:S(2)}) copy-start(bf16[128,1024]{1,0:T(8,128)(2,1)S(1)} %get-tuple-element.72) | copy-start | bytes 786436
  317.7 128.8 %copy-start.18 = (bf16[128,1024]{1,0:T(8,128)(2,1)}, bf16[128,1024]{1,0:T(8,128)(2,1)S(1)}, u32[]{:S(2)}) copy-start(bf16[128,1024]{1,0:T(8,128)(2,1)S(1)} %get-tuple-element.70) | copy-start | bytes 786436
  320.5 5.3 copy-start.24
  321.2 125.3 %copy-start.20 = (bf16[128,1024]{1,0:T(8,128)(2,1)}, bf16[128,1024]{1,0:T(8,128)(2,1)S(1)}, u32[]{:S(2)}) copy-start(bf16[128,1024]{1,0:T(8,128)(2,1)S(1)} %get-tuple-element.68) | copy-start | bytes 786436
  330.3 160.6 %all-reduce.14.cloned.1.call-start = ((), (), s32[]{:S(2)}) async-start(), calls=%async_computation.3 | async-start | bytes 2097152 | tf_op jit(solution)/shard_map/psum | solution.py:30
  446.2 581.8 %all-reduce.16.cloned.1.call-start = ((), (), s32[]{:S(2)}) async-start(), calls=%async_computation.4 | async-start | bytes 6291456 | tf_op jit(solution)/shard_map/psum | solution.py:53
  490.9 2.6 copy-start.4
  645.4 11.5 %copy-start.11 = (bf16[128,2048]{1,0:T(8,128)(2,1)}, bf16[128,2048]{1,0:T(8,128)(2,1)S(1)}, u32[]{:S(2)}) copy-start(bf16[128,2048]{1,0:T(8,128)(2,1)S(1)} %get-tuple-element.80) | copy-start | bytes 1572868
  645.4 3.6 copy-start.1
  648.9 7.9 copy-start.12
  652.3 4.6 copy-start.13
  652.3 5.1 copy-start.25
  656.6 2.4 copy-start.23
  659.0 2.4 copy-start.17
  659.0 2.4 copy-start.19
  659.0 2.4 copy-start.21
  1031.6 10.5 copy-start.6
  1042.0 3.2 copy-start.7
  1042.0 3.2 copy-start.15
  (7 other events, 8.9 us)
Sparse Core Ops, SparseCore 0:
  14.7 61.0 all-reduce.7
  81.0 87.8 all-reduce.9
  330.4 107.8 all-reduce.11
  446.4 44.5 all-reduce.13
  665.3 362.7 all-reduce.15
where the time goes:
time: 1060 us
  waiting for transfers between devices  662 us (62%)
  other arithmetic  247 us (23%)
  matrix products  95.3 us (9%)
  local copies, waits for them, and re-layouts  35.5 us (3%)
  between operations  19.7 us (2%)
    psum x1, waiting for transfers between devices, per_device(): lax.psum((core_part, turn_left_part, turn_right_part), ('row', 'col'))  363 us
    another operation x29, other arithmetic, solve_rows(): factor = jnp.linalg.cholesky(gram)  162 us
    psum x1, waiting for transfers between devices, per_device(): right_image = lax.psum(right_part, 'row')  108 us
    psum x1, waiting for transfers between devices, per_device(): left_gram = lax.psum(gram_of(left_image), 'row')  87.5 us
    another operation x7, other arithmetic, solve_rows(): jax.scipy.linalg.solve_triangular(factor, image.T, lower=True)  81.5 us
    psum x1, waiting for transfers between devices, per_device(): lax.psum(jnp.dot(grad, right_old, preferred_element_type=jnp.float32), 'c...  61.2 us
    psum x1, waiting for transfers between devices, per_device(): right_gram = lax.psum(gram_of(right_image), 'col')  42.1 us
    another operation x14, matrix products, solve_rows(): jax.scipy.linalg.solve_triangular(factor, image.T, lower=True)  26.1 us
  transfers between devices with their start and end apart: 5, of which 5 were waited for; matrix products, arithmetic and copies ran while one was open for 0% of the time, Pallas kernels for 0%

commit v1 on v0

--- a/solution.py
+++ b/solution.py
@@ -23,7 +23,9 @@
     highest = lax.Precision.HIGHEST
     across = (((0,), (0,)), ((), ()))
     left_image = lax.psum(jnp.dot(grad, right_old, preferred_element_type=jnp.float32), "col")
-    left_gram = lax.psum(gram_of(left_image), "row")
+    x = gram_of(left_image)
+    shards = lax.all_gather(x, "row")
+    left_gram = jnp.sum(shards, axis=0)
     left_basis = solve_rows(left_image, left_gram)
     right_part = lax.dot_general(grad, left_basis, across, preferred_element_type=jnp.float32)
     right_image = lax.psum(right_part, "row")

time: 1060 us -> 1090 us (1.028)
  waiting for transfers between devices: 662 us -> 682 us
    all_gather x0 -> x1, waiting for transfers between devices: none -> 108 us  [per_device(): shards = lax.all_gather(x, 'row')]
    psum x1 -> x0, waiting for transfers between devices: 87.5 us -> none  [per_device(): left_gram = lax.psum(gram_of(left_image), 'row')]
where the time goes in v1:
time: 1090 us; the launch traced here: 1080 us
  waiting for transfers between devices  682 us (63%)
  other arithmetic  251 us (23%)
  matrix products  95.3 us (9%)
  local copies, waits for them, and re-layouts  34.2 us (3%)
  between operations  19.9 us (2%)
    psum x1, waiting for transfers between devices, per_device(): lax.psum((core_part, turn_left_part, turn_right_part), ('row', 'col'))  363 us
    another operation x29, other arithmetic, solve_rows(): factor = jnp.linalg.cholesky(gram)  163 us
    all_gather x1, waiting for transfers between devices, per_device(): shards = lax.all_gather(x, 'row')  108 us
    psum x1, waiting for transfers between devices, per_device(): right_image = lax.psum(right_part, 'row')  108 us
    another operation x7, other arithmetic, solve_rows(): jax.scipy.linalg.solve_triangular(factor, image.T, lower=True)  81.1 us
    psum x1, waiting for transfers between devices, per_device(): lax.psum(jnp.dot(grad, right_old, preferred_element_type=jnp.float32), 'c...  61.2 us
    psum x1, waiting for transfers between devices, per_device(): right_gram = lax.psum(gram_of(right_image), 'col')  42.3 us
    another operation x14, matrix products, solve_rows(): jax.scipy.linalg.solve_triangular(factor, image.T, lower=True)  26.1 us
  transfers between devices with their start and end apart: 5, of which 5 were waited for; matrix products, arithmetic and copies ran while one was open for 0% of the time, Pallas kernels for 0%

profile of v1, /device:TPU:0, one launch (start us, length us, event | category | flops | bytes accessed | tf_op | source)
XLA Modules:
  0.0 1083.9 jit_solution(17705203934913090651)
XLA Ops:
  14.7 61.2 %all-reduce.7.cloned.1.call-done = f32[1024,512]{1,0:T(8,128)} async-done(((f32[1024,512]{1,0:T(8,128)}), f32[1024,512]{1,0:T(8,128)}) %all-reduce.7.cloned.1.call-update) | async-done | bytes 2097168 | tf_op jit(solution)/shard_map/psum | solution.py:25
  81.4 107.9 %all-gather.3.cloned.1.call-done = f32[4096,512]{1,0:T(8,128)} async-done(((f32[512,512]{1,0:T(8,128)}), f32[4096,512]{1,0:T(8,128)}) %all-gather.3.cloned.1.call-update) | async-done | bytes 8388624 | tf_op jit(solution)/shard_map/all_gather | solution.py:27
  197.6 11.7 %cholesky.286 = f32[128,128]{1,0:T(8,128)S(1)} custom-call(f32[128,128]{1,0:T(8,128)S(1)} %cholesky.426), custom_call_target="Cholesky" | custom-call | tf_op jit(solution)/shard_map/jit(cholesky)/cholesky | solution.py:8
  209.5 9.8 custom-call.33
  221.8 11.8 %cholesky.305 = f32[128,128]{1,0:T(8,128)S(1)} custom-call(f32[128,128]{1,0:T(8,128)S(1)} %cholesky.430), custom_call_target="Cholesky" | custom-call | tf_op jit(solution)/shard_map/jit(cholesky)/cholesky | solution.py:8
  233.7 9.8 custom-call.34
  245.0 11.7 %cholesky.326 = f32[128,128]{1,0:T(8,128)S(1)} custom-call(f32[128,128]{1,0:T(8,128)S(1)} %cholesky.435), custom_call_target="Cholesky" | custom-call | tf_op jit(solution)/shard_map/jit(cholesky)/cholesky | solution.py:8
  256.8 9.8 custom-call.35
  268.1 12.1 %cholesky.343 = f32[128,128]{1,0:T(8,128)S(1)} custom-call(f32[128,128]{1,0:T(8,128)S(1)} %convolution_subtract_fusion.9), custom_call_target="Cholesky" | custom-call | tf_op jit(solution)/shard_map/jit(cholesky)/cholesky | solution.py:8
  285.8 11.6 %while.2 = (s32[]{:T(128)}, f32[512,512]{1,0:T(8,128)}, s32[4,2]{0,1:T(2,128)S(1)}, f32[4,128,128]{2,1,0:T(8,128)S(1)}, s32[]{:T(128)}) while((s32[]{:T(128)}, f32[512,512]{1,0:T(8,128)}, s32[4,2]{0,1:T(2,128)S(1)}, f32[4,128,128]{2,1,0:T(8,128)S(1)}, s32[]{:T(128)}) %tuple.61), condition=%wide.while_cond, body=%wide.while_body.sunk | while | flops 2 | bytes 131189 | solution.py:9
  297.4 39.3 %custom-call.28 = f32[4,128,128]{1,2,0:T(8,128)S(1)} custom-call(f32[4,128,128]{2,1,0:T(8,128)S(1)} %get-tuple-element.12), custom_call_target="InvertDiagBlocksLowerTriangular" | custom-call | tf_op jit(solution)/shard_map/jit(_solve_triangular)/triangular_solve | solution.py:9
  354.2 107.6 %all-reduce.9.cloned.1.call-done = f32[2048,512]{0,1:T(8,128)} async-done(((f32[2048,512]{0,1:T(8,128)}), f32[2048,512]{0,1:T(8,128)}) %all-reduce.9.cloned.1.call-update) | async-done | bytes 4194320 | tf_op jit(solution)/shard_map/psum | solution.py:31
  472.1 42.3 %all-reduce.11.cloned.1.call-done = f32[512,512]{0,1:T(8,128)} async-done(((f32[512,512]{0,1:T(8,128)}), f32[512,512]{0,1:T(8,128)}) %all-reduce.11.cloned.1.call-update) | async-done | bytes 1048592 | tf_op jit(solution)/shard_map/psum | solution.py:32
  519.5 11.7 %cholesky.358 = f32[128,128]{1,0:T(8,128)S(1)} custom-call(f32[128,128]{1,0:T(8,128)S(1)} %cholesky.439), custom_call_target="Cholesky" | custom-call | tf_op jit(solution)/shard_map/jit(cholesky)/cholesky | solution.py:8
  531.4 9.8 custom-call.36
  544.4 11.7 %cholesky.377 = f32[128,128]{1,0:T(8,128)S(1)} custom-call(f32[128,128]{1,0:T(8,128)S(1)} %cholesky.443), custom_call_target="Cholesky" | custom-call | tf_op jit(solution)/shard_map/jit(cholesky)/cholesky | solution.py:8
  556.2 10.2 custom-call.37
  569.5 13.2 %cholesky.398 = f32[128,128]{1,0:T(8,128)} custom-call(f32[128,128]{1,0:T(8,128)} %cholesky.448), custom_call_target="Cholesky" | custom-call | tf_op jit(solution)/shard_map/jit(cholesky)/cholesky | solution.py:8
  584.1 11.3 %custom-call.38 = f32[1,128,128]{1,2,0:T(8,128)} custom-call(f32[1,128,128]{2,1,0:T(8,128)} %get-tuple-element.49), custom_call_target="InvertDiagBlocksLowerTriangular" | custom-call | tf_op jit(solution)/shard_map/jit(cholesky)/cholesky | solution.py:8
  597.7 11.9 %cholesky.415 = f32[128,128]{1,0:T(8,128)S(1)} custom-call(f32[128,128]{1,0:T(8,128)S(1)} %convolution_subtract_fusion.8), custom_call_target="Cholesky" | custom-call | tf_op jit(solution)/shard_map/jit(cholesky)/cholesky | solution.py:8
  615.9 11.6 %while.3 = (s32[]{:T(128)}, f32[512,512]{1,0:T(8,128)}, s32[4,2]{0,1:T(2,128)S(1)}, f32[4,128,128]{2,1,0:T(8,128)S(1)}, s32[]{:T(128)}) while((s32[]{:T(128)}, f32[512,512]{1,0:T(8,128)}, s32[4,2]{0,1:T(2,128)S(1)}, f32[4,128,128]{2,1,0:T(8,128)S(1)}, s32[]{:T(128)}) %tuple.78), condition=%wide.while_cond.1, body=%wide.while_body.1.sunk | while | flops 2 | bytes 131189 | solution.py:9
  627.5 39.3 %custom-call.29 = f32[4,128,128]{1,2,0:T(8,128)S(1)} custom-call(f32[4,128,128]{2,1,0:T(8,128)S(1)} %get-tuple-element.20), custom_call_target="InvertDiagBlocksLowerTriangular" | custom-call | tf_op jit(solution)/shard_map/jit(_solve_triangular)/triangular_solve | solution.py:9
  688.9 363.1 %all-reduce.13.cloned.1.call-done = (f32[512,512]{1,0:T(8,128)}, f32[512,512]{1,0:T(8,128)}, f32[512,512]{1,0:T(8,128)}) async-done(((f32[512,512]{1,0:T(8,128)}, f32[512,512]{1,0:T(8,128)}, f32[512,512]{1,0:T(8,128)}), (f32[512,512]{1,0:T(8,128)}, f32[512,512]{1,0:T(8,128)}, f32[512,512]{1,0:T(8,128)})) %all-reduce.13.cloned.1.call-update) | async-done | bytes 3145744 | tf_op jit(solution)/shard_map/psum | solution.py:55
  1055.5 10.4 subtract_convert_fusion
  (160 shorter events, 136.2 us)
Async XLA Ops:
  7.2 68.7 %all-reduce.7.cloned.1.call-start = ((), (), s32[]{:S(2)}) async-start(), calls=%async_computation | async-start | bytes 4194304 | tf_op jit(solution)/shard_map/psum | solution.py:25
  14.6 174.8 %all-gather.3.cloned.1.call-start = ((), (), s32[]{:S(2)}) async-start(), calls=%async_computation.3 | async-start | bytes 9437184 | tf_op jit(solution)/shard_map/all_gather | solution.py:27
  80.9 380.9 %all-reduce.9.cloned.1.call-start = ((), (), s32[]{:S(2)}) async-start(), calls=%async_computation.1 | async-start | bytes 8388608 | tf_op jit(solution)/shard_map/psum | solution.py:31
  336.7 4.7 copy-start.2
  338.6 131.2 %copy-start.15 = (bf16[128,1024]{1,0:T(8,128)(2,1)}, bf16[128,1024]{1,0:T(8,128)(2,1)S(1)}, u32[]{:S(2)}) copy-start(bf16[128,1024]{1,0:T(8,128)(2,1)S(1)} %get-tuple-element.72) | copy-start | bytes 786436
  341.4 128.4 %copy-start.17 = (bf16[128,1024]{1,0:T(8,128)(2,1)}, bf16[128,1024]{1,0:T(8,128)(2,1)S(1)}, u32[]{:S(2)}) copy-start(bf16[128,1024]{1,0:T(8,128)(2,1)S(1)} %get-tuple-element.70) | copy-start | bytes 786436
  344.2 5.3 copy-start.23
  344.9 124.9 %copy-start.19 = (bf16[128,1024]{1,0:T(8,128)(2,1)}, bf16[128,1024]{1,0:T(8,128)(2,1)S(1)}, u32[]{:S(2)}) copy-start(bf16[128,1024]{1,0:T(8,128)(2,1)S(1)} %get-tuple-element.68) | copy-start | bytes 786436
  354.0 160.4 %all-reduce.11.cloned.1.call-start = ((), (), s32[]{:S(2)}) async-start(), calls=%async_computation.2 | async-start | bytes 2097152 | tf_op jit(solution)/shard_map/psum | solution.py:32
  469.7 582.3 %all-reduce.13.cloned.1.call-start = ((), (), s32[]{:S(2)}) async-start(), calls=%async_computation.4 | async-start | bytes 6291456 | tf_op jit(solution)/shard_map/psum | solution.py:55
  514.5 2.6 copy-start.4
  669.1 11.5 %copy-start.10 = (bf16[128,2048]{1,0:T(8,128)(2,1)}, bf16[128,2048]{1,0:T(8,128)(2,1)S(1)}, u32[]{:S(2)}) copy-start(bf16[128,2048]{1,0:T(8,128)(2,1)S(1)} %get-tuple-element.80) | copy-start | bytes 1572868
  669.1 3.6 copy-start.1
  672.7 7.9 copy-start.11
  676.1 4.6 copy-start.12
  676.1 5.1 copy-start.24
  680.3 2.4 copy-start.22
  682.7 2.4 copy-start.16
  682.7 2.4 copy-start.18
  682.7 2.4 copy-start.20
  1055.5 10.4 copy-start.5
  1065.9 3.2 copy-start.6
  1065.9 3.2 copy-start.14
  1069.2 2.0 copy-start.3
  (6 other events, 6.9 us)
Sparse Core Ops, SparseCore 0:
  14.7 61.0 all-reduce.6
  81.0 108.2 all-gather.2
  354.1 107.6 all-reduce.8
  469.9 44.5 all-reduce.10
  689.0 362.9 all-reduce.12
